TPU v7x, 32 devices: a whole 2x2x4 slice. The times are simulated.
32 devices in a mesh: res: 4 (over x, core), blk: 8 (over z, y).
Axes of the slice: x: 2, y: 2, z: 4, core: 2. Of those that a mesh axis runs over, the one named last changes fastest.
Arguments:
- modes: float32 [2, 8, 4194304], P(None, 'res', 'blk'), may hold values from -0.078125 to 0.078125
Outputs:
- product_modes: float32 [2, 8, 4194304], P(None, 'res', 'blk')
All inputs are finite; a program needn't handle non-finite values.
Results may differ from a plain program's by a relative error of at most 0.000098.
Values sent between devices are 32-bit elements; how exact they have to be, the bound alone decides.
A program may use at most 192 MiB of HBM per device.

v0:
```python
import math

import jax
import jax.numpy as jnp
from jax import lax
from jax.sharding import PartitionSpec as P

INNER = 512
EIGHTH = 4194304
SUBLEN = 12582912
PADDED = 50331648


highest = lax.Precision.HIGHEST


def grid_index(shape, axis_number):
    return lax.broadcasted_iota(jnp.int32, shape, axis_number)


def rotation(position, period, direction, factor):
    angle = direction * 2.0 * math.pi / period * (position % period).astype(jnp.float32)
    return jnp.stack([factor * jnp.cos(angle), factor * jnp.sin(angle)])


def times(left, right):
    return jnp.stack(
        [left[0] * right[0] - left[1] * right[1], left[0] * right[1] + left[1] * right[0]]
    )


def table_pair(length):
    rows = grid_index((length, length), 0)
    columns = grid_index((length, length), 1)
    angle = 2.0 * math.pi / length * (rows * columns % length).astype(jnp.float32)
    cosine = jnp.cos(angle)
    sine = jnp.sin(angle)
    forward = jnp.stack([jnp.stack([cosine, -sine], 1), jnp.stack([sine, cosine], 1)])
    backward = jnp.stack([jnp.stack([cosine, sine], 1), jnp.stack([-sine, cosine], 1)])
    return (forward, backward)


def fold_eighths(every, residue):
    parity = residue % 2
    quarter = jnp.stack([(1 - parity) * (1 - residue), parity * (2 - residue)]).astype(jnp.float32)
    quarter = quarter.reshape((2,) + (1,) * (every.ndim - 1))
    flipped = (1 - 2 * parity).astype(jnp.float32)
    padding = jnp.zeros_like(every[:, 0:1])
    upper = jnp.concatenate([every[:, 6:8], padding], axis=1)
    return every[:, 0:3] + times(quarter, every[:, 3:6]) + flipped * upper


def on_device(modes):
    width = modes.shape[2]
    blocks = lax.axis_size("blk")
    block = lax.axis_index("blk")
    residue = lax.axis_index("res")
    narrow = width // blocks
    outer = width // INNER
    first_len = 3 * blocks
    first_pair = table_pair(first_len)
    outer_pair = table_pair(outer)
    inner_pair = table_pair(INNER)
    moved_in = lax.all_to_all(
        modes.reshape(2, 2, blocks, narrow), "blk", split_axis=2, concat_axis=2, tiled=True
    )
    every = lax.all_gather(moved_in, "res", axis=1, tiled=True)
    shape = (3, blocks, narrow)
    position = (
        EIGHTH * grid_index(shape, 0)
        + width * grid_index(shape, 1)
        + block * narrow
        + grid_index(shape, 2)
    )
    spread = times(rotation(residue * position, PADDED, 1.0, 1.0), fold_eighths(every, residue))
    gathered = spread.reshape(2, first_len, narrow)
    section = jnp.einsum("akbj,bjr->akr", first_pair[0], gathered, precision=highest)
    freq_ids = grid_index((first_len, narrow), 0)
    column_ids = block * narrow + grid_index((first_len, narrow), 1)
    section = times(rotation(freq_ids * column_ids, SUBLEN, 1.0, 1.0), section)
    back = lax.all_to_all(
        section.reshape(2, blocks, 3, narrow), "blk", split_axis=1, concat_axis=3, tiled=True
    )
    local = back.reshape(2, 3, outer, INNER)
    local = jnp.einsum("asbp,bxpc->axsc", outer_pair[0], local, precision=highest)
    inner_turn = rotation(
        grid_index((outer, INNER), 0) * grid_index((outer, INNER), 1), width, 1.0, 1.0
    )
    inner_turn = inner_turn.reshape(2, 1, outer, INNER)
    local = times(inner_turn, local)
    values = jnp.einsum("akbj,bxsj->axsk", inner_pair[0], local, precision=highest)
    squared = jnp.stack(
        [values[0] * values[0] - values[1] * values[1], 2.0 * values[0] * values[1]]
    )
    local = jnp.einsum("akbj,bxsj->axsk", inner_pair[1], squared, precision=highest)
    local = times(jnp.stack([inner_turn[0], -inner_turn[1]]), local)
    local = jnp.einsum("asbp,bxpc->axsc", outer_pair[1], local, precision=highest).reshape(
        2, 3, width
    )
    slab_ids = 3 * block + grid_index((3, width), 0)
    local = times(rotation(slab_ids * grid_index((3, width), 1), SUBLEN, -1.0, 1.0), local)
    moved = lax.all_to_all(
        local.reshape(2, 3, blocks, narrow), "blk", split_axis=2, concat_axis=1, tiled=True
    )
    inverted = jnp.einsum(
        "akbj,bjr->akr", first_pair[1], moved.reshape(2, first_len, narrow), precision=highest
    )
    home = lax.all_to_all(
        inverted.reshape(2, 3, blocks, narrow), "blk", split_axis=2, concat_axis=3, tiled=True
    )
    home = home.reshape(2, 3, width)
    picked = jnp.concatenate([home[:, 1:3], home, home], axis=1)
    place = (grid_index((8, width), 0) + 4) * EIGHTH + block * width + grid_index((8, width), 1)
    partial_value = times(rotation(residue * place, PADDED, -1.0, 1.0 / PADDED), picked)
    return lax.psum_scatter(partial_value, "res", scatter_dimension=1, tiled=True)


def solution(mesh):
    return jax.shard_map(
        on_device,
        mesh=mesh,
        in_specs=(P(None, "res", "blk"),),
        out_specs=P(None, "res", "blk"),
        check_vma=False,
    )
```

profile of v0, /device:TPU:0, one launch (start us, length us, event | category | flops | bytes accessed | tf_op | source)
XLA Modules:
  0.0 2739.0 jit_solution(15947584154978163904)
XLA Ops:
  11.0 190.2 %all_to_all.44 = f32[2,2,8,65536]{3,1,0,2:T(2,128)S(1)} all-to-all(f32[2,2,8,65536]{3,1,0,2:T(2,128)S(1)} %bitcast.138), channel_id=1, replica_groups=mesh['res'=4,'blk'=8] {'blk'}, dimensions={2} | all-to-all | bytes 16777216 | tf_op jit(solution)/shard_map/all_to_all | solution.py:64
  210.4 199.7 %all-gather.2.cloned.1.call-done = f32[2,8,8,65536]{3,2,1,0:T(8,128)} async-done(((f32[2,2,8,65536]{3,2,1,0:T(8,128)}), f32[2,8,8,65536]{3,2,1,0:T(8,128)}) %all-gather.2.cloned.1.call-update) | async-done | bytes 33554448 | tf_op jit(solution)/shard_map/all_gather | solution.py:67
  429.5 27.5 %subtract_bitcast_fusion = (f32[1,24,65536]{2,1,0:T(8,128)S(1)}, f32[1,24,65536]{2,1,0:T(8,128)S(1)}) fusion(f32[2,3,8,65536]{3,2,1,0:T(8,128)S(1)} %fusion.11, s32[]{:T(128)S(6)} %mul.723, s32[8]{0:T(128)S(1)} %iota_multiply_fusion, s32[3]{0:T(128)S(1)} %iota_multiply_fusion.1, s32[]{:T(128)S(6)} %axis_index.23), kind=kLoop, calls=%fused_computation.75 | loop fusion | flops 28311552 | bytes 25165876 | tf_op jit(solution)/shard_map/stack | solution.py:27
  468.2 28.1 %multiply_subtract_fusion.5 = (f32[1,24,65536]{2,1,0:T(8,128)}, f32[1,24,65536]{2,1,0:T(8,128)}) fusion(f32[2,24,65536]{2,1,0:T(8,128)S(1)} %convolution_bitcast_fusion.1, s32[65536]{0:T(1024)S(1)} %iota_add_fusion), kind=kLoop, calls=%fused_computation.73 | loop fusion | flops 23592960 | bytes 25427968 | tf_op jit(solution)/shard_map/sub | solution.py:28
  567.1 17.7 fusion.72
  584.7 16.5 fusion.77
  601.2 22.5 fusion.26
  623.7 186.8 %all-to-all-done.1 = f32[2,8,3,65536]{3,0,2,1:T(2,128)} async-done(((f32[2,8,3,65536]{3,0,2,1:T(2,128)}), f32[2,8,3,65536]{3,0,2,1:T(2,128)}, u32[]{:S(2)}, u32[]{:S(2)}) %all-to-all-start.1) | async-done | bytes 12582944 | tf_op jit(solution)/shard_map/all_to_all | solution.py:81
  810.5 16.4 copy.57
  837.9 163.0 %fusion.45 = f32[2,3,1024,512]{2,3,0,1:T(8,128)} fusion(f32[1,1024,2,1024]{3,1,2,0:T(8,128)} %get-tuple-element.28, f32[1,1024,2,1024]{3,1,2,0:T(8,128)} %get-tuple-element.23, f32[2,3,1024,512]{3,2,1,0:T(8,128)} %reshape.608), kind=kOutput, calls=%fused_computation.92 | convolution fusion | flops 77313605632 | bytes 41943040 | tf_op jit(solution)/shard_map/asbp,bxpc->axsc/dot_general | solution.py:85
  1006.7 98.2 %fusion.49 = f32[2,3,1024,512]{3,2,0,1:T(8,128)S(1)} fusion(f32[1,3,1024,512]{2,3,0,1:T(8,128)S(1)} %get-tuple-element.12, f32[1,3,1024,512]{2,3,0,1:T(8,128)S(1)} %get-tuple-element.11, f32[1,512,2,512]{3,1,2,0:T(8,128)} %get-tuple-element.30, f32[1,512,2,512]{3,1,2,0:T(8,128)} %get-tuple-element.33), kind=kOutput, calls=%fused_computation.94 | convolution fusion | flops 38658899968 | bytes 29360128 | tf_op jit(solution)/shard_map/akbj,bxsj->axsk/dot_general | solution.py:91
  1108.5 43.1 %fusion.48 = f32[2,3,1024,512]{2,3,0,1:T(8,128)S(1)} fusion(f32[1,3,1024,512]{3,2,0,1:T(8,128)} %get-tuple-element.22, f32[1,3,1024,512]{3,2,0,1:T(8,128)S(1)} %get-tuple-element.21, f32[1,512,2,512]{3,1,2,0:T(8,128)} %get-tuple-element.34, f32[1,512,2,512]{3,1,2,0:T(8,128)} %get-tuple-element.29), kind=kOutput, calls=%fused_computation.93 | convolution fusion | flops 38658899968 | bytes 29360128 | tf_op jit(solution)/shard_map/akbj,bxsj->axsk/dot_general | solution.py:95
  1157.4 88.3 %fusion.50 = f32[2,3,1024,512]{2,3,0,1:T(8,128)} fusion(f32[1,1024,2,1024]{3,1,2,0:T(8,128)} %get-tuple-element.24, f32[1,1024,2,1024]{3,1,2,0:T(8,128)} %get-tuple-element.27, f32[1,3,1024,512]{2,3,0,1:T(8,128)} %get-tuple-element.10, f32[1,3,1024,512]{2,3,0,1:T(8,128)} %get-tuple-element.9), kind=kOutput, calls=%fused_computation.95 | convolution fusion | flops 77316751360 | bytes 41943040 | tf_op jit(solution)/shard_map/asbp,bxpc->axsc/dot_general | solution.py:97
  1284.7 31.1 %multiply_subtract_fusion.1 = (f32[1,3,8,65536]{3,2,1,0:T(8,128)S(1)}, f32[1,3,8,65536]{3,2,1,0:T(8,128)}) fusion(f32[1,3,8,65536]{3,2,1,0:T(8,128)} %squeeze.5, f32[1,3,8,65536]{3,2,1,0:T(8,128)} %squeeze.4, s32[3]{0:T(128)S(1)} %copy-done.2), kind=kLoop, calls=%fused_computation.62 | loop fusion | flops 26738688 | bytes 25165836 | tf_op jit(solution)/shard_map/sub | solution.py:28
  1323.9 21.9 copy.63
  1351.4 272.4 %all-to-all-done.2 = f32[2,3,8,65536]{3,0,1,2:T(2,128)} async-done(((f32[2,3,8,65536]{3,0,1,2:T(2,128)}), f32[2,3,8,65536]{3,0,1,2:T(2,128)}, u32[]{:S(2)}, u32[]{:S(2)}) %all-to-all-start.2) | async-done | bytes 12582944 | tf_op jit(solution)/shard_map/all_to_all | solution.py:102
  1623.8 22.7 convolution_bitcast_fusion
  1663.1 271.5 %all-to-all-done.3 = f32[2,3,8,65536]{3,0,1,2:T(2,128)} async-done(((f32[2,3,8,65536]{3,0,1,2:T(2,128)}), f32[2,3,8,65536]{3,0,1,2:T(2,128)}, u32[]{:S(2)}, u32[]{:S(2)}) %all-to-all-start.3) | async-done | bytes 12582944 | tf_op jit(solution)/shard_map/all_to_all | solution.py:108
  1950.9 21.6 reshape.628
  1982.9 20.1 pad_maximum_fusion
  2003.1 76.4 %multiply_subtract_fusion = (f32[1,8,524288]{2,1,0:T(8,128)}, f32[1,8,524288]{2,1,0:T(8,128)}) fusion(f32[2,8,524288]{2,1,0:T(8,128)S(1)} %pad_maximum_fusion, s32[8]{0:T(128)S(1)} %multiply_add_fusion.7, s32[]{:T(128)S(6)} %axis_index.23), kind=kLoop, calls=%fused_computation.16 | loop fusion | flops 75497472 | bytes 67108896 | tf_op jit(solution)/shard_map/sub | solution.py:28
  2079.5 22.4 pad_maximum_fusion.1
  2101.9 54.7 %copy.70 = f32[2,8,524288]{2,0,1:T(2,128)} copy(f32[2,8,524288]{2,1,0:T(8,128)} %pad_maximum_fusion.1) | data formatting | bytes 67108864 | tf_op jit(solution)/shard_map/stack | solution.py:27
  2158.5 554.8 %all-reduce.4.cloned.1.call-done = f32[2,8,524288]{2,0,1:T(2,128)} async-done(((f32[2,8,524288]{2,0,1:T(2,128)}), f32[2,8,524288]{2,0,1:T(2,128)}) %all-reduce.4.cloned.1.call-update) | async-done | bytes 33554448
  (58 shorter events, 256.8 us)
Async XLA Ops:
  6.5 403.6 %all-gather.2.cloned.1.call-start = ((), (), s32[]{:S(2)}) async-start(), calls=%async_computation.4 | async-start | bytes 41943040 | tf_op jit(solution)/shard_map/all_gather | solution.py:67
  410.1 10.2 slice-start
  531.1 279.4 %all-to-all-start.1 = ((f32[2,8,3,65536]{3,0,2,1:T(2,128)}), f32[2,8,3,65536]{3,0,2,1:T(2,128)}, u32[]{:S(2)}, u32[]{:S(2)}) async-start(f32[2,8,3,65536]{3,0,2,1:T(2,128)} %pad_maximum_fusion.2), calls=%async_computation.1 | async-start | bytes 25165824 | tf_op jit(solution)/shard_map/all_to_all | solution.py:81
  837.9 163.0 %copy-start.1 = (f32[1024,512]{0,1:T(8,128)S(1)}, f32[1024,512]{0,1:T(8,128)}, u32[]{:S(2)}) copy-start(f32[1024,512]{0,1:T(8,128)} %get-tuple-element.46) | copy-start | bytes 6291460
  1108.4 43.1 %copy-start = (f32[1024,512]{0,1:T(8,128)S(1)}, f32[1024,512]{0,1:T(8,128)}, u32[]{:S(2)}) copy-start(f32[1024,512]{0,1:T(8,128)} %fusion.86) | copy-start | bytes 6291460
  1277.9 6.8 copy-start.2
  1345.9 277.9 %all-to-all-start.2 = ((f32[2,3,8,65536]{3,0,1,2:T(2,128)}), f32[2,3,8,65536]{3,0,1,2:T(2,128)}, u32[]{:S(2)}, u32[]{:S(2)}) async-start(f32[2,3,8,65536]{3,0,1,2:T(2,128)} %copy.63), calls=%async_computation.2 | async-start | bytes 25165824 | tf_op jit(solution)/shard_map/all_to_all | solution.py:102
  1657.5 277.1 %all-to-all-start.3 = ((f32[2,3,8,65536]{3,0,1,2:T(2,128)}), f32[2,3,8,65536]{3,0,1,2:T(2,128)}, u32[]{:S(2)}, u32[]{:S(2)}) async-start(f32[2,3,8,65536]{3,0,1,2:T(2,128)} %copy.65), calls=%async_computation.3 | async-start | bytes 25165824 | tf_op jit(solution)/shard_map/all_to_all | solution.py:108
  1662.8 1050.5 %all-reduce.4.cloned.1.call-start = ((), (), s32[]{:S(2)}) async-start(), calls=%async_computation.5 | async-start | bytes 67108864
  2156.6 0.7 copy-start.3
Sparse Core Ops, SparseCore 0:
  209.6 200.4 all-gather.1
  2156.8 556.5 all-reduce.3
where the time goes:
time: 2750 us; the launch traced here: 2740 us
  waiting for transfers between devices  1490 us (54%)
  matrix products  427 us (16%)
  other arithmetic  349 us (13%)
  local copies, waits for them, and re-layouts  257 us (9%)
  blocking collectives  190 us (7%)
    unnamed x3, waiting for transfers between devices  555 us
    all_to_all x1, waiting for transfers between devices, on_device(): lax.all_to_all(local.reshape(2, 3, blocks, narrow), 'blk', split_axis=2,...  272 us
    all_to_all x1, waiting for transfers between devices, on_device(): lax.all_to_all(inverted.reshape(2, 3, blocks, narrow), 'blk', split_axis=...  271 us
    all_gather x1, waiting for transfers between devices, on_device(): every = lax.all_gather(moved_in, 'res', axis=1, tiled=True)  200 us
    all_to_all x1, blocking collectives, on_device(): lax.all_to_all(modes.reshape(2, 2, blocks, narrow), 'blk', split_axis=2,...  190 us
    all_to_all x1, waiting for transfers between devices, on_device(): lax.all_to_all(section.reshape(2, blocks, 3, narrow), 'blk', split_axis=1...  187 us
    dot_general x1, matrix products, on_device(): jnp.einsum('asbp,bxpc->axsc', outer_pair[0], local, precision=highest)  163 us
    sub x6, other arithmetic, times(): left[0] * right[0] - left[1] * right[1]  157 us
  transfers between devices with their start and end apart: 5, of which 5 were waited for; matrix products, arithmetic and copies ran while one was open for 3% of the time, Pallas kernels for 0%

commit v1 on v0

v1 whole, which is shorter than its diff:
```python
import math

import jax
import jax.numpy as jnp
from jax import lax
from jax.sharding import PartitionSpec as P

INNER = 512

high = lax.Precision.HIGH


def turn(numerator, period):
    angle = 2.0 * math.pi / period * (numerator % period).astype(jnp.float32)
    return jnp.cos(angle), jnp.sin(angle)


def times(left, right):
    return (left[0] * right[0] - left[1] * right[1], left[0] * right[1] + left[1] * right[0])


def conj(pair):
    return (pair[0], -pair[1])


def gauss_tables(length, zero):
    rows = lax.broadcasted_iota(jnp.int32, (length, length), 0) + zero
    columns = lax.broadcasted_iota(jnp.int32, (length, length), 1)
    cosine, sine = turn(rows * columns, length)
    return cosine, sine + cosine, sine - cosine


def dot(left, right):
    return jnp.dot(left, right, precision=high)


def forward_dft(multiply, tables, value):
    base = multiply(tables[0], value[0] + value[1])
    return (base - multiply(tables[1], value[1]), base + multiply(tables[2], value[0]))


def backward_dft(multiply, tables, value):
    base = multiply(tables[0], value[0] + value[1])
    return (base + multiply(tables[2], value[1]), base - multiply(tables[1], value[0]))


def from_left(table, value):
    return dot(table, value)


def from_right(table, value):
    return dot(value, table)


def on_device(modes):
    own, width = modes.shape[1:]
    blocks = lax.axis_size("blk")
    residues = lax.axis_size("res")
    block = lax.axis_index("blk")
    residue = lax.axis_index("res")
    narrow = width // blocks
    inner = min(INNER, width // 8)
    outer = width // inner
    eighths = own * residues
    period = residues * 3 * blocks
    padded = period * width
    zero = residue // (16 * residues)

    def swap(value, bit):
        return lax.ppermute(value, "res", [(q, q ^ bit) for q in range(residues)])

    def sections(owners, offset):
        shape = (3, blocks, 2, len(owners), 2, own, blocks)
        ids = [lax.broadcasted_iota(jnp.int32, shape, i) for i in range(7)]
        owner = sum(
            jnp.where(ids[3] == i, o, 0) for i, o in enumerate(owners)
        )
        freq = residues * (3 * ids[1] + ids[0]) + residue
        place = (own * owner + ids[5] + offset) * blocks + ids[6]
        cosine, sine = turn(freq * place, period)
        return jnp.where(ids[2] == ids[4], cosine, jnp.where(ids[2] == 0, -sine, sine))

    outer_tables = gauss_tables(outer, zero)
    inner_tables = gauss_tables(inner, zero)
    row_ids = lax.broadcasted_iota(jnp.int32, (outer, 1), 0) + zero
    column_ids = lax.broadcasted_iota(jnp.int32, (1, inner), 1)
    inner_turn = turn(row_ids * column_ids, width)

    moved_in = lax.all_to_all(
        modes.reshape(2, own, blocks, narrow), "blk", split_axis=2, concat_axis=2, tiled=True
    )
    mine = moved_in.reshape(2 * own * blocks, narrow)
    across = swap(mine, 2)
    beside = swap(mine, 1)
    diagonal = swap(across, 1)
    every = jnp.concatenate([mine, beside, across, diagonal], axis=0)
    order = [residue, residue ^ 1, residue ^ 2, residue ^ 3]
    matrix = sections(order, 0).reshape(3, 2 * blocks, 2 * own * blocks * residues)

    returned = []
    for slab in range(3):
        section = dot(matrix[slab], every).reshape(blocks, 2, narrow // 128, 128)
        back = lax.all_to_all(section, "blk", split_axis=0, concat_axis=0, tiled=True)
        local = (back[:, 0].reshape(outer, inner), back[:, 1].reshape(outer, inner))
        freq = residues * (3 * block + slab) + residue
        row_turn = turn(freq * (inner * row_ids), padded)
        column_turn = turn(freq * column_ids, padded)
        local = times(row_turn, times(column_turn, local))
        local = forward_dft(from_left, outer_tables, local)
        local = times(inner_turn, local)
        local = forward_dft(from_right, inner_tables, local)
        local = (local[0] * local[0] - local[1] * local[1], 2.0 * local[0] * local[1])
        local = backward_dft(from_right, inner_tables, local)
        local = times(conj(inner_turn), local)
        local = backward_dft(from_left, outer_tables, local)
        local = times(conj(row_turn), times(conj(column_turn), local))
        packed = jnp.stack(
            [part.reshape(blocks, narrow // 128, 128) for part in local], axis=1
        )
        moved = lax.all_to_all(packed, "blk", split_axis=0, concat_axis=0, tiled=True)
        returned.append(moved.reshape(2 * blocks, narrow))
    spectrum = jnp.concatenate(returned, axis=0)

    def share(owners):
        table = sections(owners, eighths // 2) * (1.0 / padded)
        table = table.reshape(6 * blocks, 2 * own * blocks * len(owners))
        return lax.dot_general(
            table, spectrum, (((0,), (0,)), ((), ())), precision=high
        )

    half = 2 * own * blocks
    given = swap(share([residue ^ 1, residue ^ 3]), 1)
    kept = share([residue, residue ^ 2])
    given_across = swap(kept[half:] + given[half:], 2)
    total = kept[:half] + given[:half] + given_across
    home = lax.all_to_all(
        total.reshape(2, own, blocks, narrow), "blk", split_axis=2, concat_axis=2, tiled=True
    )
    return home.reshape(2, own, width)


def solution(mesh):
    return jax.shard_map(
        on_device,
        mesh=mesh,
        in_specs=(P(None, "res", "blk"),),
        out_specs=P(None, "res", "blk"),
        check_vma=False,
    )
```

time: 2750 us -> 1990 us (0.72)
  waiting for transfers between devices: 1490 us -> 614 us
  matrix products: 427 us -> 651 us
  other arithmetic: 349 us -> 153 us
  blocking collectives: 190 us -> 377 us
  local copies, waits for them, and re-layouts: 257 us -> 147 us
    unnamed x3 -> x0, waiting for transfers between devices: 555 us -> none
    all_to_all x3 -> x6, waiting for transfers between devices: 731 us -> 230 us  [the longest x3 171 us: on_device(): lax.all_to_all(packed, 'blk', split_axis=0, concat_axis=0, tiled=True)]
    ppermute x0 -> x5, waiting for transfers between devices: none -> 384 us  [swap(): return lax.ppermute(value, 'res', [(q, q ^ bit) for q in range(residues)])]
    dot_general x6 -> x41, matrix products: 427 us -> 651 us  [the longest x39 624 us: dot(): return jnp.dot(left, right, precision=high)]
    all_gather x1 -> x0, waiting for transfers between devices: 200 us -> none  [on_device(): every = lax.all_gather(moved_in, 'res', axis=1, tiled=True)]
    all_to_all x1 -> x2, blocking collectives: 190 us -> 377 us  [the longest x1 190 us: on_device(): lax.all_to_all(modes.reshape(2, own, blocks, narrow), 'blk', split_axis=2...]
    sub x6 -> x3, other arithmetic: 157 us -> 28.9 us  [times(): left[0] * right[0] - left[1] * right[1]]
    dot_general x0 -> x13, other arithmetic: none -> 90.1 us  [dot(): return jnp.dot(left, right, precision=high)]
  transfers between devices with their start and end apart: 5 -> 11, of which waited for: 5 -> 7; matrix products, arithmetic and copies ran while one was open for 3% -> 35% of each run, Pallas kernels for 0% -> 0%
where the time goes in v1:
time: 1990 us; the launch traced here: 1980 us
  matrix products  651 us (33%)
  waiting for transfers between devices  614 us (31%)
  blocking collectives  377 us (19%)
  other arithmetic  153 us (8%)
  local copies, waits for them, and re-layouts  147 us (7%)
  starting transfers between devices  35.7 us (2%)
    dot_general x39, matrix products, dot(): return jnp.dot(left, right, precision=high)  624 us
    ppermute x5, waiting for transfers between devices, swap(): return lax.ppermute(value, 'res', [(q, q ^ bit) for q in range(residues)])  384 us
    all_to_all x1, blocking collectives, on_device(): lax.all_to_all(modes.reshape(2, own, blocks, narrow), 'blk', split_axis=2...  190 us
    all_to_all x1, blocking collectives, on_device(): lax.all_to_all(total.reshape(2, own, blocks, narrow), 'blk', split_axis=2...  186 us
    all_to_all x3, waiting for transfers between devices, on_device(): lax.all_to_all(packed, 'blk', split_axis=0, concat_axis=0, tiled=True)  171 us
    dot_general x13, other arithmetic, dot(): return jnp.dot(left, right, precision=high)  90.1 us
    all_to_all x3, waiting for transfers between devices, on_device(): lax.all_to_all(section, 'blk', split_axis=0, concat_axis=0, tiled=True)  59.6 us
    dot_general x7, local copies, waits for them, and re-layouts, dot(): return jnp.dot(left, right, precision=high)  49 us
  transfers between devices with their start and end apart: 11, of which 7 were waited for; matrix products, arithmetic and copies ran while one was open for 35% of the time, Pallas kernels for 0%

profile of v1, /device:TPU:0, one launch (start us, length us, event | category | flops | bytes accessed | tf_op | source)
XLA Modules:
  0.0 1978.4 jit_solution(4492513196239416173)
XLA Ops:
  4.5 190.2 %all_to_all.40 = f32[2,2,8,65536]{3,1,0,2:T(2,128)S(1)} all-to-all(f32[2,2,8,65536]{3,1,0,2:T(2,128)S(1)} %bitcast.82), channel_id=1, replica_groups=mesh['res'=4,'blk'=8] {'blk'}, dimensions={2} | all-to-all | bytes 16777216 | tf_op jit(solution)/shard_map/all_to_all | solution.py:89
  204.4 179.8 %collective-permute-done.1 = f32[32,65536]{1,0:T(8,128)} collective-permute-done((f32[32,65536]{1,0:T(8,128)}, f32[32,65536]{1,0:T(8,128)}, u32[]{:S(2)}, u32[]{:S(2)}) %collective-permute-start.1) | collective-permute-done | bytes 8388640 | tf_op jit(solution)/shard_map/ppermute | solution.py:70
  397.7 22.7 %maximum_bitcast_fusion = f32[65536,128]{0,1:T(8,128)} fusion(f32[32,65536]{1,0:T(8,128)} %collective-permute-done.2, f32[32,65536]{1,0:T(8,128)} %collective-permute-done.1, f32[32,65536]{1,0:T(8,128)} %collective-permute-done, f32[32,65536]{1,0:T(8,128)} %bitcast.1), kind=kLoop, calls=%fused_computation | loop fusion | flops 25165824 | bytes 67108864 | tf_op jit(solution)/shard_map/dot_general | solution.py:34
  420.5 33.4 %copy.30 = f32[65536,128]{1,0:T(8,128)} copy(f32[65536,128]{0,1:T(8,128)} %maximum_bitcast_fusion) | data formatting | bytes 67108864 | tf_op jit(solution)/shard_map/dot_general | solution.py:34
  453.9 20.5 %fusion.185 = f32[8,2,512,128]{3,0,2,1:T(8,128)} fusion(f32[512,128,128,1]{2,1,0,3:T(8,128)} %bitcast.78, f32[8,2,128,1]{2,0,1,3:T(8,128)S(1)} %reshape.261), kind=kOutput, calls=%fused_computation.204 | convolution fusion | flops 805306368 | bytes 37756928 | tf_op jit(solution)/shard_map/dot_general | solution.py:34
  492.9 20.3 %fusion.183 = f32[8,2,512,128]{3,0,2,1:T(8,128)} fusion(f32[512,128,128,1]{2,1,0,3:T(8,128)} %bitcast.79, f32[8,2,128,1]{2,0,1,3:T(8,128)S(1)} %reshape.263), kind=kOutput, calls=%fused_computation.202 | convolution fusion | flops 805306368 | bytes 37756928 | tf_op jit(solution)/shard_map/dot_general | solution.py:34
  518.2 59.6 %all-to-all-done.1 = f32[8,2,512,128]{3,2,1,0:T(8,128)} async-done(((f32[8,2,512,128]{3,2,1,0:T(8,128)}), f32[8,2,512,128]{3,2,1,0:T(8,128)}, u32[]{:S(2)}, u32[]{:S(2)}) %all-to-all-start.1) | async-done | bytes 4194336 | tf_op jit(solution)/shard_map/all_to_all | solution.py:103
  582.7 20.3 %fusion.181 = f32[8,2,512,128]{3,0,2,1:T(8,128)} fusion(f32[512,128,128,1]{2,1,0,3:T(8,128)} %bitcast.80, f32[8,2,128,1]{2,0,1,3:T(8,128)S(1)} %reshape.264), kind=kOutput, calls=%fused_computation.200 | convolution fusion | flops 805306368 | bytes 37756928 | tf_op jit(solution)/shard_map/dot_general | solution.py:34
  640.2 20.5 %fusion.71 = f32[1024,512]{1,0:T(8,128)S(1)} fusion(f32[1024,512]{1,0:T(8,128)S(1)} %fusion.32, s32[1024]{0:T(1024)S(1)} %iota_add_fusion.2, f32[1024,512]{1,0:T(8,128)S(1)} %multiply_subtract_fusion.48), kind=kOutput, calls=%fused_computation.126 | convolution fusion | flops 3237478400 | bytes 6295552 | tf_op jit(solution)/shard_map/dot_general | solution.py:34
  742.1 21.2 %fusion.24 = f32[1024,512]{1,0:T(8,128)S(1)} fusion(s32[1024]{0:T(1024)S(1)} %iota_add_fusion.2, f32[1024]{0:T(1024)S(1)} %get-tuple-element.26, f32[1024]{0:T(1024)S(1)} %get-tuple-element.27, f32[1024,512]{1,0:T(8,128)S(1)} %reshape_squeeze.21, f32[512]{0:T(512)S(1)} %get-tuple-element.30, f32[1024,512]{1,0:T(8,128)} %reshape_squeeze.20, ...), kind=kOutput, calls=%fused_computation.64 | convolution fusion | flops 3242721280 | bytes 6307840 | tf_op jit(solution)/shard_map/dot_general | solution.py:34
  764.8 20.5 %fusion.77 = f32[1024,512]{1,0:T(8,128)S(1)} fusion(f32[1024,512]{1,0:T(8,128)S(1)} %fusion.24, s32[1024]{0:T(1024)S(1)} %iota_add_fusion.2, f32[1024,512]{1,0:T(8,128)S(1)} %multiply_subtract_fusion.49), kind=kOutput, calls=%fused_computation.128 | convolution fusion | flops 3237478400 | bytes 6295552 | tf_op jit(solution)/shard_map/dot_general | solution.py:34
  785.3 20.3 %fusion.95 = f32[1024,512]{1,0:T(8,128)S(1)} fusion(f32[1024,512]{1,0:T(8,128)S(1)} %fusion.24, s32[1024]{0:T(1024)S(1)} %iota_add_fusion.2, f32[1024,512]{1,0:T(8,128)S(1)} %multiply_add_fusion.47), kind=kOutput, calls=%fused_computation.134 | convolution fusion | flops 3237478400 | bytes 6295552 | tf_op jit(solution)/shard_map/dot_general | solution.py:34
  954.7 22.6 %fusion.16 = f32[1024,512]{1,0:T(8,128)} fusion(s32[1024]{0:T(1024)S(1)} %iota_add_fusion.2, f32[1024]{0:T(1024)S(1)} %copy-done.20, f32[1024]{0:T(1024)S(1)} %copy-done.15, f32[1024,512]{1,0:T(8,128)S(1)} %reshape_squeeze.23, f32[512]{0:T(512)S(1)} %copy-done.26, f32[1024,512]{1,0:T(8,128)} %reshape_squeeze.22, f32[512]{0:T(512)S(1)} %copy-done.21), kind=kOutput, calls=%fused_computation.42 | convolution fusion | flops 3242721280 | bytes 6307840 | tf_op jit(solution)/shard_map/dot_general | solution.py:34
  1000.3 20.2 %fusion.74 = f32[1024,512]{1,0:T(8,128)S(1)} fusion(f32[1024,512]{1,0:T(8,128)S(1)} %fusion.26, s32[1024]{0:T(1024)S(1)} %iota_add_fusion.2, f32[1024,512]{1,0:T(8,128)S(1)} %copy-done.13), kind=kOutput, calls=%fused_computation.127 | convolution fusion | flops 3237478400 | bytes 6295552 | tf_op jit(solution)/shard_map/dot_general | solution.py:34
  1020.6 23.0 %multiply_subtract_fusion.14 = (f32[1024,512]{1,0:T(8,128)}, f32[1024,512]{1,0:T(8,128)}) fusion(f32[1024]{0:T(1024)S(1)} %copy-done.33, f32[1024]{0:T(1024)S(1)} %copy-done.19, f32[512]{0:T(512)S(1)} %copy-done.37, f32[1024,512]{1,0:T(8,128)S(1)} %fusion.74, f32[512]{0:T(512)S(1)} %copy-done.25, f32[1024,512]{1,0:T(8,128)S(1)} %fusion.26, ...), kind=kOutput, calls=%fused_computation.71 | convolution fusion | flops 3243769856 | bytes 10502144 | tf_op jit(solution)/shard_map/dot_general | solution.py:34
  1076.6 20.4 %fusion.83 = f32[1024,512]{1,0:T(8,128)S(1)} fusion(f32[1024,512]{1,0:T(8,128)S(1)} %copy-done.43, s32[1024]{0:T(1024)S(1)} %iota_add_fusion.2, f32[1024,512]{1,0:T(8,128)S(1)} %copy-done.8), kind=kOutput, calls=%fused_computation.130 | convolution fusion | flops 3237478400 | bytes 6295552 | tf_op jit(solution)/shard_map/dot_general | solution.py:34
  1117.1 20.4 %fusion.80 = f32[1024,512]{1,0:T(8,128)S(1)} fusion(f32[1024,512]{1,0:T(8,128)S(1)} %fusion.18, s32[1024]{0:T(1024)S(1)} %iota_add_fusion.2, f32[1024,512]{1,0:T(8,128)S(1)} %copy-done.10), kind=kOutput, calls=%fused_computation.129 | convolution fusion | flops 3237478400 | bytes 6295552 | tf_op jit(solution)/shard_map/dot_general | solution.py:34
  1137.5 23.4 %multiply_subtract_fusion.7 = (f32[1024,512]{1,0:T(8,128)}, f32[1024,512]{1,0:T(8,128)}) fusion(f32[1024]{0:T(1024)S(1)} %copy-done.32, f32[1024]{0:T(1024)S(1)} %copy-done.17, f32[512]{0:T(512)S(1)} %copy-done.36, f32[1024,512]{1,0:T(8,128)S(1)} %fusion.80, f32[512]{0:T(512)S(1)} %copy-done.23, f32[1024,512]{1,0:T(8,128)S(1)} %fusion.18, ...), kind=kOutput, calls=%fused_computation.49 | convolution fusion | flops 3243769856 | bytes 10502144 | tf_op jit(solution)/shard_map/dot_general | solution.py:34
  1277.5 20.4 %fusion.86 = f32[1024,512]{1,0:T(8,128)S(1)} fusion(f32[1024,512]{1,0:T(8,128)S(1)} %fusion.10, s32[1024]{0:T(1024)S(1)} %iota_add_fusion.2, f32[1024,512]{1,0:T(8,128)S(1)} %multiply_add_fusion.45), kind=kOutput, calls=%fused_computation.131 | convolution fusion | flops 3237478400 | bytes 6295552 | tf_op jit(solution)/shard_map/dot_general | solution.py:34
  1297.8 23.0 %multiply_subtract_fusion = (f32[1024,512]{1,0:T(8,128)}, f32[1024,512]{1,0:T(8,128)}) fusion(f32[1024]{0:T(1024)S(1)} %copy-done.31, f32[1024]{0:T(1024)S(1)} %copy-done.15, f32[512]{0:T(512)S(1)} %copy-done.35, f32[1024,512]{1,0:T(8,128)S(1)} %fusion.86, f32[512]{0:T(512)S(1)} %copy-done.21, f32[1024,512]{1,0:T(8,128)S(1)} %fusion.10, ...), kind=kOutput, calls=%fused_computation.27 | convolution fusion | flops 3243769856 | bytes 10502144 | tf_op jit(solution)/shard_map/dot_general | solution.py:34
  1345.3 84.6 %all-to-all-done.4 = f32[8,2,512,128]{3,2,1,0:T(8,128)} async-done(((f32[8,2,512,128]{3,2,1,0:T(8,128)}), f32[8,2,512,128]{3,2,1,0:T(8,128)}, u32[]{:S(2)}, u32[]{:S(2)}) %all-to-all-start.4) | async-done | bytes 4194336 | tf_op jit(solution)/shard_map/all_to_all | solution.py:120
  1441.3 85.9 %all-to-all-done.6 = f32[8,2,512,128]{3,2,1,0:T(8,128)} async-done(((f32[8,2,512,128]{3,2,1,0:T(8,128)}), f32[8,2,512,128]{3,2,1,0:T(8,128)}, u32[]{:S(2)}, u32[]{:S(2)}) %all-to-all-start.6) | async-done | bytes 4194336 | tf_op jit(solution)/shard_map/all_to_all | solution.py:120
  1584.5 181.2 %collective-permute-done.4 = f32[32,65536]{1,0:T(8,128)S(1)} collective-permute-done((f32[32,65536]{1,0:T(8,128)}, f32[32,65536]{1,0:T(8,128)S(1)}, u32[]{:S(2)}, u32[]{:S(2)}) %collective-permute-start.4) | collective-permute-done | bytes 8388640 | tf_op jit(solution)/shard_map/ppermute | solution.py:70
  1787.2 186.4 %all_to_all.41 = f32[2,2,8,65536]{3,1,0,2:T(2,128)S(1)} all-to-all(f32[2,2,8,65536]{3,1,0,2:T(2,128)S(1)} %copy.40), channel_id=1, replica_groups=mesh['res'=4,'blk'=8] {'blk'}, dimensions={2} | all-to-all | bytes 16777216 | tf_op jit(solution)/shard_map/all_to_all | solution.py:136
  (211 shorter events, 636.5 us)
Async XLA Ops:
  202.9 181.3 %collective-permute-start.1 = (f32[32,65536]{1,0:T(8,128)}, f32[32,65536]{1,0:T(8,128)}, u32[]{:S(2)}, u32[]{:S(2)}) collective-permute-start(f32[32,65536]{1,0:T(8,128)} %bitcast.1), channel_id=1, source_target_pairs={{0,16},{8,24},{16,0},{24,8},{1,17},{9,25},{17,1},{25,9},{2,18},{10... | collective-permute-start | bytes 25165832 | tf_op jit(solution)/shard_map/ppermute | solution.py:70
  204.4 182.1 %collective-permute-start = (f32[32,65536]{1,0:T(8,128)}, f32[32,65536]{1,0:T(8,128)}, u32[]{:S(2)}, u32[]{:S(2)}) collective-permute-start(f32[32,65536]{1,0:T(8,128)} %bitcast.1), channel_id=1, source_target_pairs={{0,8},{8,0},{16,24},{24,16},{1,9},{9,1},{17,25},{25,17},{2,10},{10... | collective-permute-start | bytes 25165832 | tf_op jit(solution)/shard_map/ppermute | solution.py:70
  384.2 13.5 collective-permute-start.2
  479.3 98.6 %all-to-all-start.1 = ((f32[8,2,512,128]{3,2,1,0:T(8,128)}), f32[8,2,512,128]{3,2,1,0:T(8,128)}, u32[]{:S(2)}, u32[]{:S(2)}) async-start(f32[8,2,512,128]{3,2,1,0:T(8,128)} %copy.31), calls=%async_computation.1 | async-start | bytes 8388608 | tf_op jit(solution)/shard_map/all_to_all | solution.py:103
  490.0 130.6 %copy-start.24 = (f32[512]{0:T(512)}, f32[512]{0:T(512)S(1)}, u32[]{:S(2)}) copy-start(f32[512]{0:T(512)S(1)} %get-tuple-element.21) | copy-start | bytes 6148
  490.1 274.0 %copy-start.22 = (f32[512]{0:T(512)}, f32[512]{0:T(512)S(1)}, u32[]{:S(2)}) copy-start(f32[512]{0:T(512)S(1)} %get-tuple-element.31) | copy-start | bytes 6148
  491.5 129.2 %copy-start.18 = (f32[1024]{0:T(1024)}, f32[1024]{0:T(1024)S(1)}, u32[]{:S(2)}) copy-start(f32[1024]{0:T(1024)S(1)} %get-tuple-element.23) | copy-start | bytes 12292
  492.2 271.9 %copy-start.16 = (f32[1024]{0:T(1024)}, f32[1024]{0:T(1024)S(1)}, u32[]{:S(2)}) copy-start(f32[1024]{0:T(1024)S(1)} %get-tuple-element.27) | copy-start | bytes 12292
  577.8 148.8 %all-to-all-start.3 = ((f32[8,2,512,128]{3,2,1,0:T(8,128)}), f32[8,2,512,128]{3,2,1,0:T(8,128)}, u32[]{:S(2)}, u32[]{:S(2)}) async-start(f32[8,2,512,128]{3,2,1,0:T(8,128)} %copy.34), calls=%async_computation.3 | async-start | bytes 8388608 | tf_op jit(solution)/shard_map/all_to_all | solution.py:103
  726.6 218.6 %all-to-all-start.5 = ((f32[8,2,512,128]{3,2,1,0:T(8,128)}), f32[8,2,512,128]{3,2,1,0:T(8,128)}, u32[]{:S(2)}, u32[]{:S(2)}) async-start(f32[8,2,512,128]{3,2,1,0:T(8,128)} %copy.37), calls=%async_computation.5 | async-start | bytes 8388608 | tf_op jit(solution)/shard_map/all_to_all | solution.py:103
  742.1 21.2 %copy-start.1 = (f32[1024,512]{1,0:T(8,128)S(1)}, f32[1024,512]{1,0:T(8,128)}, u32[]{:S(2)}) copy-start(f32[1024,512]{1,0:T(8,128)} %reshape_squeeze.20) | copy-start | bytes 6291460
  954.7 22.6 %copy-start.2 = (f32[1024,512]{1,0:T(8,128)S(1)}, f32[1024,512]{1,0:T(8,128)}, u32[]{:S(2)}) copy-start(f32[1024,512]{1,0:T(8,128)} %reshape_squeeze.22) | copy-start | bytes 6291460
  1051.8 280.8 %all-to-all-start.2 = ((f32[8,2,512,128]{3,2,1,0:T(8,128)}), f32[8,2,512,128]{3,2,1,0:T(8,128)}, u32[]{:S(2)}, u32[]{:S(2)}) async-start(f32[8,2,512,128]{3,2,1,0:T(8,128)} %pad_maximum_fusion), calls=%async_computation.2 | async-start | bytes 8388608 | tf_op jit(solution)/shard_map/all_to_all | solution.py:120
  1097.0 63.9 %copy-start.38 = (f32[1024,512]{1,0:T(8,128)}, f32[1024,512]{1,0:T(8,128)S(1)}, u32[]{:S(2)}) copy-start(f32[1024,512]{1,0:T(8,128)S(1)} %fusion.83) | copy-start | bytes 6291460
  1117.0 43.9 %copy-start.40 = (f32[1024,512]{1,0:T(8,128)}, f32[1024,512]{1,0:T(8,128)S(1)}, u32[]{:S(2)}) copy-start(f32[1024,512]{1,0:T(8,128)S(1)} %fusion.101) | copy-start | bytes 6291460
  1117.0 20.4 %copy-start.9 = (f32[1024,512]{1,0:T(8,128)S(1)}, f32[1024,512]{1,0:T(8,128)}, u32[]{:S(2)}) copy-start(f32[1024,512]{1,0:T(8,128)} %multiply_subtract_fusion.35.clone.2) | copy-start | bytes 6291460
  1117.0 20.4 %copy-start.17 = (f32[1024]{0:T(1024)S(1)}, f32[1024]{0:T(1024)}, u32[]{:S(2)}) copy-start(f32[1024]{0:T(1024)} %copy-done.16) | copy-start | bytes 12292
  1117.0 20.4 %copy-start.23 = (f32[512]{0:T(512)S(1)}, f32[512]{0:T(512)}, u32[]{:S(2)}) copy-start(f32[512]{0:T(512)} %copy-done.22) | copy-start | bytes 6148
  1117.0 20.4 %copy-start.32 = (f32[1024]{0:T(1024)S(1)}, f32[1024]{0:T(1024)}, u32[]{:S(2)}) copy-start(f32[1024]{0:T(1024)} %get-tuple-element.29) | copy-start | bytes 12292
  1117.0 20.4 %copy-start.36 = (f32[512]{0:T(512)S(1)}, f32[512]{0:T(512)}, u32[]{:S(2)}) copy-start(f32[512]{0:T(512)} %fusion.233) | copy-start | bytes 6148
  1332.6 97.3 %all-to-all-start.4 = ((f32[8,2,512,128]{3,2,1,0:T(8,128)}), f32[8,2,512,128]{3,2,1,0:T(8,128)}, u32[]{:S(2)}, u32[]{:S(2)}) async-start(f32[8,2,512,128]{3,2,1,0:T(8,128)} %pad_maximum_fusion.1), calls=%async_computation.4 | async-start | bytes 8388608 | tf_op jit(solution)/shard_map/all_to_all | solution.py:120
  1429.9 97.3 %all-to-all-start.6 = ((f32[8,2,512,128]{3,2,1,0:T(8,128)}), f32[8,2,512,128]{3,2,1,0:T(8,128)}, u32[]{:S(2)}, u32[]{:S(2)}) async-start(f32[8,2,512,128]{3,2,1,0:T(8,128)} %pad_maximum_fusion.2), calls=%async_computation.6 | async-start | bytes 8388608 | tf_op jit(solution)/shard_map/all_to_all | solution.py:120
  1547.5 25.5 %collective-permute-start.3 = (f32[64,65536]{1,0:T(8,128)}, f32[64,65536]{1,0:T(8,128)}, u32[]{:S(2)}, u32[]{:S(2)}) collective-permute-start(f32[64,65536]{1,0:T(8,128)} %fusion.143), channel_id=1, source_target_pairs={{0,8},{8,0},{16,24},{24,16},{1,9},{9,1},{17,25},{25,17},{2,10},{10... | collective-permute-start | bytes 50331656 | tf_op jit(solution)/shard_map/ppermute | solution.py:70
  1583.0 182.7 %collective-permute-start.4 = (f32[32,65536]{1,0:T(8,128)}, f32[32,65536]{1,0:T(8,128)S(1)}, u32[]{:S(2)}, u32[]{:S(2)}) collective-permute-start(f32[32,65536]{1,0:T(8,128)} %slice_add_fusion), channel_id=1, source_target_pairs={{0,16},{8,24},{16,0},{24,8},{1,17},{9,25},{17,1},{25,9},{2,18},{10... | collective-permute-start | bytes 25165832 | tf_op jit(solution)/shard_map/ppermute | solution.py:70
  (31 other events, 384.7 us)
